TPU v7x, 32 devices: a whole 2x2x4 slice. The times are simulated.
32 devices in a mesh: section: 4 (over z), tensor: 8 (over y, x, core).
Axes of the slice: x: 2, y: 2, z: 4, core: 2. Of those that a mesh axis runs over, the one named last changes fastest.
Arguments:
- resid: bfloat16 [32, 3584], P('tensor'), may hold values from -6 to 6
- w_enc: bfloat16 [7168, 3584], P(('section', 'tensor')), may hold values from -0.09375 to 0.09375
- b_enc: float32 [7168], P(('section', 'tensor')), may hold values from -1 to 0.5
- w_dec: bfloat16 [7168, 3584], P(('section', 'tensor')), may hold values from -0.0625 to 0.0625
- b_dec: float32 [3584], replicated, may hold values from -3 to 3
Outputs:
- recon: float32 [32, 3584], P('tensor')
- grad_w_dec: bfloat16 [7168, 3584], P(('section', 'tensor'))
- code_grad: float32 [32, 7168], P(None, ('section', 'tensor'))
- grad_b_dec: float32 [3584], replicated
- loss_value: float32 [], replicated
All inputs are finite; a program needn't handle non-finite values.
Results may differ from a plain program's by a relative error of at most 0.0032.
The roundings to bfloat16 on the way count: a program that leaves them out, or rounds other values in their place, can miss the bound.
Values may be sent and summed in bfloat16 or wider, within the bound.
No kernel may reach another device: no remote copies, remote signals or barrier semaphores. Data moves between devices by JAX's collectives and lax.ppermute only.
A program may use at most 64 MiB of HBM per device.

v0:
```python
import jax
import jax.numpy as jnp
from jax import lax
from jax.sharding import PartitionSpec as P

epsilon = 1e-06


def per_device(resid, w_enc, b_enc, w_dec, b_dec):
    stream = lax.all_gather(resid, "tensor", axis=0, tiled=True)
    preact = (
        lax.dot_general(stream, w_enc, (((1,), (1,)), ((), ())), preferred_element_type=jnp.float32)
        + b_enc
    )
    codes = jnp.maximum(preact, 0.0).astype(jnp.bfloat16)
    codes_f32 = codes.astype(jnp.float32)
    dec_f32 = w_dec.astype(jnp.float32)
    dec_norm = jnp.sqrt(jnp.sum(dec_f32 * dec_f32, axis=1) + epsilon)
    penalty = lax.psum(jnp.sum(codes_f32 * dec_norm), ("section", "tensor"))
    total_rows = stream.shape[0]
    model_width = stream.shape[1]
    shares = lax.psum_scatter(
        jnp.dot(codes, w_dec, preferred_element_type=jnp.float32),
        "tensor",
        scatter_dimension=0,
        tiled=True,
    )
    shares = lax.psum(shares, "section")
    recon = shares + b_dec
    errors = recon - resid.astype(jnp.float32)
    squares, grad_b_dec = lax.psum((jnp.sum(errors * errors), jnp.sum(errors, axis=0)), "tensor")
    err_half = lax.all_gather(errors.astype(jnp.bfloat16), "tensor", axis=0, tiled=True)
    loss_value = (0.5 * squares + penalty) / (total_rows * model_width)
    code_sums = jnp.sum(codes_f32, axis=0)
    grad_w_dec = lax.dot_general(
        codes, err_half, (((0,), (0,)), ((), ())), preferred_element_type=jnp.float32
    )
    grad_w_dec = grad_w_dec + code_sums[:, None] * dec_f32 / dec_norm[:, None]
    code_grad = (
        lax.dot_general(
            err_half, w_dec, (((1,), (1,)), ((), ())), preferred_element_type=jnp.float32
        )
        + dec_norm
    )
    return (recon, grad_w_dec.astype(jnp.bfloat16), code_grad, grad_b_dec, loss_value)


def solution(mesh):
    in_specs = (
        P("tensor", None),
        P(("section", "tensor"), None),
        P(("section", "tensor")),
        P(("section", "tensor"), None),
        P(),
    )
    out_specs = (
        P("tensor", None),
        P(("section", "tensor"), None),
        P(None, ("section", "tensor")),
        P(),
        P(),
    )
    return jax.shard_map(
        per_device, mesh=mesh, in_specs=in_specs, out_specs=out_specs, check_vma=False
    )
```

profile of v0, /device:TPU:0, one launch (start us, length us, event | category | flops | bytes accessed | tf_op | source)
XLA Modules:
  0.0 148.7 jit_solution(17115211651597049739)
XLA Ops:
  7.2 0.0 copy-start
  7.2 0.0 copy-start.2
  7.2 0.0 copy-start.6
  7.2 0.0 all-reduce.4.cloned.1.call-start
  7.2 1.9 %fusion.2 = f32[224]{0:T(256)S(1)} fusion(bf16[224,3584]{1,0:T(8,128)(2,1)} %param.8), kind=kLoop, calls=%fused_computation.5 | loop fusion | flops 2408224 | bytes 1606528 | tf_op jit(solution)/shard_map/reduce_sum | solution.py:18
  9.2 0.0 copy-start.1
  9.2 0.0 copy-done.2
  9.2 12.0 %all-gather = bf16[8,4,3584]{2,1,0:T(4,128)(2,1)} all-gather(bf16[1,4,3584]{2,1,0:T(4,128)(2,1)S(1)} %bitcast.12), channel_id=1, replica_groups=mesh['section'=4,'tensor'=8] {'tensor'}, dimensions={0}, use_global_device_ids=true | all-gather | bytes 258048 | tf_op jit(solution)/shard_map/all_gather | solution.py:10
  21.2 1.0 reshape.22
  22.2 0.0 copy-done
  22.2 0.0 copy-done.6
  22.2 1.2 fusion.5
  23.4 0.0 copy-start.7
  23.4 0.0 copy-start.5
  23.4 0.0 copy-done.1
  23.4 1.2 fusion.7
  24.5 0.0 all-reduce.4.cloned.1.call-update
  24.5 39.9 %psum.31 = f32[]{:T(128)} all-reduce(f32[]{:T(128)} %get-tuple-element.7), channel_id=1, replica_groups=mesh['section'=4,'tensor'=8] {'section','tensor'}, use_global_device_ids=true, to_apply=%region_9.0 | all-reduce | flops 1 | bytes 8 | tf_op jit(solution)/shard_map/psum | solution.py:19
  64.4 0.0 copy-done.7
  64.4 0.6 dynamic-slice
  65.7 14.0 %all-reduce.4.cloned.1.call-done = f32[32,3584]{1,0:T(8,128)} async-done(((f32[32,3584]{1,0:T(8,128)}), f32[32,3584]{1,0:T(8,128)}) %all-reduce.4.cloned.1.call-update) | async-done | bytes 458768
  79.7 0.9 constant_dynamic-slice_fusion
  80.6 19.6 %psum.28 = f32[4,3584]{1,0:T(4,128)S(1)} all-reduce(f32[4,3584]{1,0:T(4,128)S(1)} %constant_dynamic-slice_fusion), channel_id=1, replica_groups=mesh['section'=4,'tensor'=8] {'section'}, use_global_device_ids=true, to_apply=%region_1.0 | all-reduce | flops 14336 | bytes 114688 | tf_op jit(solution)/shard_map/psum | solution.py:28
  100.2 0.0 copy-done.5
  100.2 0.7 multiply_reduce_fusion
  100.9 0.0 copy-start.3
  101.0 9.6 %all-gather.1 = bf16[8,4,3584]{2,1,0:T(4,128)(2,1)} all-gather(bf16[1,4,3584]{2,1,0:T(4,128)(2,1)S(1)} %convert_bitcast_fusion), channel_id=1, replica_groups=mesh['section'=4,'tensor'=8] {'tensor'}, dimensions={0}, use_global_device_ids=true | all-gather | bytes 258048 | tf_op jit(solution)/shard_map/all_gather | solution.py:32
  110.6 1.0 reshape.24
  111.6 1.2 convolution_add_fusion.1
  112.8 0.0 copy-start.4
  112.8 1.8 %fusion = bf16[224,3584]{1,0:T(8,128)(2,1)} fusion(bf16[32,224]{1,0:T(8,128)(2,1)S(1)} %get-tuple-element.12, bf16[32,3584]{1,0:T(8,128)(2,1)S(1)} %reshape.24, bf16[224,3584]{1,0:T(8,128)(2,1)S(1)} %copy-done.1, f32[224]{0:T(256)S(1)} %add_sqrt_fusion, f32[224]{0:T(256)S(1)} %get-tuple-element.8), kind=kOutput, calls=%fused_computation.1 | convolution fusion | flops 55394304 | bytes 3456768 | tf_op jit(solution)/shard_map/dot_general | solution.py:35
  114.6 0.0 copy-done.3
  114.6 0.0 copy-done.4
  114.6 24.8 %all-reduce.1 = (f32[3584]{0:T(1024)}, f32[]{:T(128)}) all-reduce(f32[3584]{0:T(1024)S(1)} %copy-done.4, f32[]{:T(128)} %get-tuple-element.5), channel_id=1, replica_groups=mesh['section'=4,'tensor'=8] {'tensor'}, use_global_device_ids=true, to_apply=%region_5.0 | all-reduce | flops 3585 | bytes 28680 | tf_op jit(solution)/shard_map/psum | solution.py:31
  (2 shorter events, 0.0 us)
Async XLA Ops:
  7.2 15.0 %copy-start = (bf16[224,3584]{1,0:T(8,128)(2,1)S(1)}, bf16[224,3584]{1,0:T(8,128)(2,1)}, u32[]{:S(2)}) copy-start(bf16[224,3584]{1,0:T(8,128)(2,1)} %param.6) | copy-start | bytes 4816900
  7.2 2.0 %copy-start.2 = (bf16[4,3584]{1,0:T(4,128)(2,1)S(1)}, bf16[4,3584]{1,0:T(4,128)(2,1)}, u32[]{:S(2)}) copy-start(bf16[4,3584]{1,0:T(4,128)(2,1)} %param.5) | copy-start | bytes 86020
  7.2 15.0 %copy-start.6 = (f32[224]{0:T(256)S(1)}, f32[224]{0:T(256)}, u32[]{:S(2)}) copy-start(f32[224]{0:T(256)} %param.7) | copy-start | bytes 2692
  7.2 72.5 %all-reduce.4.cloned.1.call-start = ((), (), s32[]{:S(2)}) async-start(), calls=%async_computation | async-start | bytes 917504
  9.2 14.2 %copy-start.1 = (bf16[224,3584]{1,0:T(8,128)(2,1)S(1)}, bf16[224,3584]{1,0:T(8,128)(2,1)}, u32[]{:S(2)}) copy-start(bf16[224,3584]{1,0:T(8,128)(2,1)} %param.8) | copy-start | bytes 4816900
  23.4 41.1 %copy-start.7 = (u32[32]{0:T(128)S(1)}, u32[32]{0:T(128)}, u32[]{:S(2)}) copy-start(u32[32]{0:T(128)} %constant.13) | copy-start | bytes 388
  23.4 76.8 %copy-start.5 = (f32[3584]{0:T(1024)S(1)}, f32[3584]{0:T(1024)}, u32[]{:S(2)}) copy-start(f32[3584]{0:T(1024)} %param.9) | copy-start | bytes 43012
  100.9 13.6 %copy-start.3 = (f32[4,3584]{1,0:T(4,128)}, f32[4,3584]{1,0:T(4,128)S(1)}, u32[]{:S(2)}) copy-start(f32[4,3584]{1,0:T(4,128)S(1)} %get-tuple-element.11) | copy-start | bytes 172036
  112.8 1.8 %copy-start.4 = (f32[3584]{0:T(1024)S(1)}, f32[3584]{0:T(1024)}, u32[]{:S(2)}) copy-start(f32[3584]{0:T(1024)} %get-tuple-element.6) | copy-start | bytes 43012
Sparse Core Ops, SparseCore 0:
  24.7 54.9 all-reduce.3
where the time goes:
time: 149 us
  blocking collectives  106 us (71%)
  between operations  17.2 us (12%)
  waiting for transfers between devices  14 us (9%)
  matrix products  5.33 us (4%)
  local copies, waits for them, and re-layouts  3.52 us (2%)
  other arithmetic  2.7 us (2%)
    psum x1, blocking collectives, per_device(): penalty = lax.psum(jnp.sum(codes_f32 * dec_norm), ('section', 'tensor'))  39.9 us
    psum x1, blocking collectives, per_device(): lax.psum((jnp.sum(errors * errors), jnp.sum(errors, axis=0)), 'tensor')  24.8 us
    psum x1, blocking collectives, per_device(): shares = lax.psum(shares, 'section')  19.6 us
    unnamed x2, waiting for transfers between devices  14 us
    all_gather x1, blocking collectives, per_device(): stream = lax.all_gather(resid, 'tensor', axis=0, tiled=True)  12 us
    all_gather x1, blocking collectives, per_device(): lax.all_gather(errors.astype(jnp.bfloat16), 'tensor', axis=0, tiled=True)  9.61 us
    unnamed x20, local copies, waits for them, and re-layouts  3.52 us
  transfers between devices with their start and end apart: 1, of which 1 were waited for; matrix products, arithmetic and copies ran while one was open for 0% of the time, Pallas kernels for 0%

commit v1 on v0

--- a/solution.py
+++ b/solution.py
@@ -7,7 +7,14 @@
 
 
 def per_device(resid, w_enc, b_enc, w_dec, b_dec):
-    stream = lax.all_gather(resid, "tensor", axis=0, tiled=True)
+    ring = [resid]
+    for hop in range(7):
+        ring.append(lax.ppermute(ring[-1], "tensor", [(dev, (dev + 1) % 8) for dev in range(8)]))
+    stream = jnp.roll(
+        jnp.concatenate(ring[::-1], axis=0),
+        (lax.axis_index("tensor") + 1) * ring[0].shape[0],
+        axis=0,
+    )
     preact = (
         lax.dot_general(stream, w_enc, (((1,), (1,)), ((), ())), preferred_element_type=jnp.float32)
         + b_enc

time: 149 us -> 171 us (1.15)
  waiting for transfers between devices: 14 us -> 42 us
  blocking collectives: 106 us -> 94.5 us
  local copies, waits for them, and re-layouts: 3.52 us -> 7.85 us
    ppermute x0 -> x7, waiting for transfers between devices: none -> 27.9 us  [per_device(): lax.ppermute(ring[-1], 'tensor', [(dev, (dev + 1) % 8) for dev in range(8)])]
    all_gather x1 -> x0, blocking collectives: 12 us -> none  [per_device(): stream = lax.all_gather(resid, 'tensor', axis=0, tiled=True)]
    concatenate x0 -> x1, local copies, waits for them, and re-layouts: none -> 5.32 us  [per_device(): jnp.roll(jnp.concatenate(ring[::-1], axis=0), (lax.axis_index('tensor') +...]
    unnamed x20 -> x17, local copies, waits for them, and re-layouts: 3.52 us -> 2.52 us
  transfers between devices with their start and end apart: 1 -> 8, of which waited for: 1 -> 8; matrix products, arithmetic and copies ran while one was open for 0% -> 1% of each run, Pallas kernels for 0% -> 0%
where the time goes in v1:
time: 171 us
  blocking collectives  94.5 us (55%)
  waiting for transfers between devices  42 us (25%)
  between operations  17.2 us (10%)
  local copies, waits for them, and re-layouts  7.85 us (5%)
  matrix products  6.28 us (4%)
  other arithmetic  2.49 us (1%)
    psum x1, blocking collectives, per_device(): penalty = lax.psum(jnp.sum(codes_f32 * dec_norm), ('section', 'tensor'))  40.5 us
    ppermute x7, waiting for transfers between devices, per_device(): lax.ppermute(ring[-1], 'tensor', [(dev, (dev + 1) % 8) for dev in range(8)])  27.9 us
    psum x1, blocking collectives, per_device(): lax.psum((jnp.sum(errors * errors), jnp.sum(errors, axis=0)), 'tensor')  24.8 us
    psum x1, blocking collectives, per_device(): shares = lax.psum(shares, 'section')  19.6 us
    unnamed x2, waiting for transfers between devices  14.1 us
    all_gather x1, blocking collectives, per_device(): lax.all_gather(errors.astype(jnp.bfloat16), 'tensor', axis=0, tiled=True)  9.61 us
    concatenate x1, local copies, waits for them, and re-layouts, per_device(): jnp.roll(jnp.concatenate(ring[::-1], axis=0), (lax.axis_index('tensor') +...  5.32 us
  transfers between devices with their start and end apart: 8, of which 8 were waited for; matrix products, arithmetic and copies ran while one was open for 1% of the time, Pallas kernels for 0%

profile of v1, /device:TPU:0, one launch (start us, length us, event | category | flops | bytes accessed | tf_op | source)
XLA Modules:
  0.0 171.0 jit_solution(4529813834119935268)
XLA Ops:
  7.2 0.0 copy-start
  7.2 0.0 copy-start.2
  7.2 0.0 copy-start.5
  7.2 0.0 all-reduce.4.cloned.1.call-start
  7.2 0.5 collective-permute-start
  7.8 4.6 %collective-permute-done = bf16[4,3584]{1,0:T(4,128)(2,1)S(1)} collective-permute-done((bf16[4,3584]{1,0:T(4,128)(2,1)}, bf16[4,3584]{1,0:T(4,128)(2,1)S(1)}, u32[]{:S(2)}, u32[]{:S(2)}) %collective-permute-start) | collective-permute-done | bytes 28704 | tf_op jit(solution)/shard_map/ppermute | solution.py:12
  12.4 0.0 collective-permute-start.1
  12.4 4.2 %collective-permute-done.1 = bf16[4,3584]{1,0:T(4,128)(2,1)S(1)} collective-permute-done((bf16[4,3584]{1,0:T(4,128)(2,1)S(1)}, bf16[4,3584]{1,0:T(4,128)(2,1)S(1)}, u32[]{:S(2)}, u32[]{:S(2)}) %collective-permute-start.1) | collective-permute-done | bytes 28704 | tf_op jit(solution)/shard_map/ppermute | solution.py:12
  16.6 0.0 collective-permute-start.2
  16.6 4.2 %collective-permute-done.2 = bf16[4,3584]{1,0:T(4,128)(2,1)S(1)} collective-permute-done((bf16[4,3584]{1,0:T(4,128)(2,1)S(1)}, bf16[4,3584]{1,0:T(4,128)(2,1)S(1)}, u32[]{:S(2)}, u32[]{:S(2)}) %collective-permute-start.2) | collective-permute-done | bytes 28704 | tf_op jit(solution)/shard_map/ppermute | solution.py:12
  20.8 0.0 collective-permute-start.3
  20.8 4.2 %collective-permute-done.3 = bf16[4,3584]{1,0:T(4,128)(2,1)S(1)} collective-permute-done((bf16[4,3584]{1,0:T(4,128)(2,1)S(1)}, bf16[4,3584]{1,0:T(4,128)(2,1)S(1)}, u32[]{:S(2)}, u32[]{:S(2)}) %collective-permute-start.3) | collective-permute-done | bytes 28704 | tf_op jit(solution)/shard_map/ppermute | solution.py:12
  25.0 0.0 collective-permute-start.4
  25.0 4.2 %collective-permute-done.4 = bf16[4,3584]{1,0:T(4,128)(2,1)S(1)} collective-permute-done((bf16[4,3584]{1,0:T(4,128)(2,1)S(1)}, bf16[4,3584]{1,0:T(4,128)(2,1)S(1)}, u32[]{:S(2)}, u32[]{:S(2)}) %collective-permute-start.4) | collective-permute-done | bytes 28704 | tf_op jit(solution)/shard_map/ppermute | solution.py:12
  29.2 0.0 collective-permute-start.5
  29.2 1.8 %fusion.2 = f32[224]{0:T(256)S(1)} fusion(bf16[224,3584]{1,0:T(8,128)(2,1)} %param.8), kind=kLoop, calls=%fused_computation.5 | loop fusion | flops 2408224 | bytes 1606528 | tf_op jit(solution)/shard_map/reduce_sum | solution.py:25
  31.0 0.0 copy-start.1
  31.0 2.4 %collective-permute-done.5 = bf16[4,3584]{1,0:T(4,128)(2,1)S(1)} collective-permute-done((bf16[4,3584]{1,0:T(4,128)(2,1)S(1)}, bf16[4,3584]{1,0:T(4,128)(2,1)S(1)}, u32[]{:S(2)}, u32[]{:S(2)}) %collective-permute-start.5) | collective-permute-done | bytes 28704 | tf_op jit(solution)/shard_map/ppermute | solution.py:12
  33.4 0.0 collective-permute-start.6
  33.4 4.2 %collective-permute-done.6 = bf16[4,3584]{1,0:T(4,128)(2,1)S(1)} collective-permute-done((bf16[4,3584]{1,0:T(4,128)(2,1)S(1)}, bf16[4,3584]{1,0:T(4,128)(2,1)S(1)}, u32[]{:S(2)}, u32[]{:S(2)}) %collective-permute-start.6) | collective-permute-done | bytes 28704 | tf_op jit(solution)/shard_map/ppermute | solution.py:12
  37.6 0.0 copy-done.2
  37.6 5.3 %concatenate.6 = bf16[64,3584]{1,0:T(8,128)(2,1)} concatenate(bf16[4,3584]{1,0:T(4,128)(2,1)S(1)} %collective-permute-done.6, bf16[4,3584]{1,0:T(4,128)(2,1)S(1)} %collective-permute-done.5, bf16[4,3584]{1,0:T(4,128)(2,1)S(1)} %collective-permute-done.4, bf16[4,3584]{1,0:T(4,128)(2,1)S(1)} %collective-permute-done.3, bf16[4,3584]{1,0:T(4,128)(2,1)S(1)} %collective-permute-done.2, ...), dimensions={0} | concatenate | bytes 917504 | tf_op jit(solution)/shard_map/jit(_roll_dynamic)/concatenate | solution.py:13
  42.9 0.0 copy-done
  42.9 0.0 copy-done.5
  42.9 2.1 %fusion.6 = (f32[]{:T(128)}, f32[224]{0:T(256)S(1)}, bf16[32,224]{1,0:T(8,128)(2,1)S(1)}) fusion(f32[224]{0:T(256)S(1)} %add_sqrt_fusion, f32[224]{0:T(256)S(1)} %copy-done.5, bf16[224,3584]{1,0:T(8,128)(2,1)S(1)} %copy-done, bf16[64,3584]{1,0:T(8,128)(2,1)} %concatenate.6, s32[]{:T(128)S(6)} %select_n.14), kind=kOutput, calls=%fused_computation.15 | convolution fusion | flops 51430176 | bytes 1852040 | tf_op jit(solution)/shard_map/dot_general | solution.py:19
  45.1 0.0 copy-start.6
  45.1 0.0 copy-start.4
  45.1 0.0 copy-done.1
  45.1 1.2 fusion.9
  46.2 0.0 all-reduce.4.cloned.1.call-update
  46.3 0.0 copy-done.6
  46.3 0.6 dynamic-slice
  47.5 40.5 %psum.31 = f32[]{:T(128)} all-reduce(f32[]{:T(128)} %get-tuple-element.7), channel_id=1, replica_groups=mesh['section'=4,'tensor'=8] {'section','tensor'}, use_global_device_ids=true, to_apply=%region_9.10 | all-reduce | flops 1 | bytes 8 | tf_op jit(solution)/shard_map/psum | solution.py:26
  88.1 14.1 %all-reduce.4.cloned.1.call-done = f32[32,3584]{1,0:T(8,128)} async-done(((f32[32,3584]{1,0:T(8,128)}), f32[32,3584]{1,0:T(8,128)}) %all-reduce.4.cloned.1.call-update) | async-done | bytes 458768
  102.2 0.9 constant_dynamic-slice_fusion
  103.1 19.6 %psum.28 = f32[4,3584]{1,0:T(4,128)S(1)} all-reduce(f32[4,3584]{1,0:T(4,128)S(1)} %constant_dynamic-slice_fusion), channel_id=1, replica_groups=mesh['section'=4,'tensor'=8] {'section'}, use_global_device_ids=true, to_apply=%region_1.2 | all-reduce | flops 14336 | bytes 114688 | tf_op jit(solution)/shard_map/psum | solution.py:35
  122.6 0.0 copy-done.4
  122.7 0.7 multiply_reduce_fusion
  123.3 0.0 copy-start.3
  123.3 9.6 %all-gather = bf16[8,4,3584]{2,1,0:T(4,128)(2,1)} all-gather(bf16[1,4,3584]{2,1,0:T(4,128)(2,1)S(1)} %convert_bitcast_fusion), channel_id=1, replica_groups=mesh['section'=4,'tensor'=8] {'tensor'}, dimensions={0}, use_global_device_ids=true | all-gather | bytes 258048 | tf_op jit(solution)/shard_map/all_gather | solution.py:39
  132.9 1.0 reshape.22
  133.9 1.2 convolution_add_fusion.1
  135.1 1.8 %fusion = bf16[224,3584]{1,0:T(8,128)(2,1)} fusion(bf16[32,224]{1,0:T(8,128)(2,1)S(1)} %get-tuple-element.12, bf16[32,3584]{1,0:T(8,128)(2,1)S(1)} %reshape.22, bf16[224,3584]{1,0:T(8,128)(2,1)S(1)} %copy-done.1, f32[224]{0:T(256)S(1)} %add_sqrt_fusion, f32[224]{0:T(256)S(1)} %get-tuple-element.8), kind=kOutput, calls=%fused_computation.1 | convolution fusion | flops 55394304 | bytes 3456768 | tf_op jit(solution)/shard_map/dot_general | solution.py:42
  136.9 0.0 copy-done.3
  136.9 24.8 %all-reduce.1 = (f32[3584]{0:T(1024)}, f32[]{:T(128)}) all-reduce(f32[3584]{0:T(1024)S(1)} %get-tuple-element.6, f32[]{:T(128)} %get-tuple-element.5), channel_id=1, replica_groups=mesh['section'=4,'tensor'=8] {'tensor'}, use_global_device_ids=true, to_apply=%region_5.6 | all-reduce | flops 3585 | bytes 28680 | tf_op jit(solution)/shard_map/psum | solution.py:38
  (2 shorter events, 0.0 us)
Async XLA Ops:
  7.2 35.8 %copy-start = (bf16[224,3584]{1,0:T(8,128)(2,1)S(1)}, bf16[224,3584]{1,0:T(8,128)(2,1)}, u32[]{:S(2)}) copy-start(bf16[224,3584]{1,0:T(8,128)(2,1)} %param.6) | copy-start | bytes 4816900
  7.2 30.4 %copy-start.2 = (bf16[4,3584]{1,0:T(4,128)(2,1)S(1)}, bf16[4,3584]{1,0:T(4,128)(2,1)}, u32[]{:S(2)}) copy-start(bf16[4,3584]{1,0:T(4,128)(2,1)} %param.5) | copy-start | bytes 86020
  7.2 35.7 %copy-start.5 = (f32[224]{0:T(256)S(1)}, f32[224]{0:T(256)}, u32[]{:S(2)}) copy-start(f32[224]{0:T(256)} %param.7) | copy-start | bytes 2692
  7.2 95.0 %all-reduce.4.cloned.1.call-start = ((), (), s32[]{:S(2)}) async-start(), calls=%async_computation | async-start | bytes 917504
  7.2 5.2 %collective-permute-start = (bf16[4,3584]{1,0:T(4,128)(2,1)}, bf16[4,3584]{1,0:T(4,128)(2,1)S(1)}, u32[]{:S(2)}, u32[]{:S(2)}) collective-permute-start(bf16[4,3584]{1,0:T(4,128)(2,1)} %param.5), channel_id=1, source_target_pairs={{0,1},{1,2},{2,3},{3,4},{4,5},{5,6},{6,7},{7,0},{8,9},{9,10},{10,1... | collective-permute-start | bytes 86024 | tf_op jit(solution)/shard_map/ppermute | solution.py:12
  12.4 4.2 %collective-permute-start.1 = (bf16[4,3584]{1,0:T(4,128)(2,1)S(1)}, bf16[4,3584]{1,0:T(4,128)(2,1)S(1)}, u32[]{:S(2)}, u32[]{:S(2)}) collective-permute-start(bf16[4,3584]{1,0:T(4,128)(2,1)S(1)} %collective-permute-done), channel_id=1, source_target_pairs={{0,1},{1,2},{2,3},{3,4},{4,5},{5,6},{6,7},{7,0},{8,9},{9,10},{10,1... | collective-permute-start | bytes 86024 | tf_op jit(solution)/shard_map/ppermute | solution.py:12
  16.6 4.2 %collective-permute-start.2 = (bf16[4,3584]{1,0:T(4,128)(2,1)S(1)}, bf16[4,3584]{1,0:T(4,128)(2,1)S(1)}, u32[]{:S(2)}, u32[]{:S(2)}) collective-permute-start(bf16[4,3584]{1,0:T(4,128)(2,1)S(1)} %collective-permute-done.1), channel_id=1, source_target_pairs={{0,1},{1,2},{2,3},{3,4},{4,5},{5,6},{6,7},{7,0},{8,9},{9,10},{10,1... | collective-permute-start | bytes 86024 | tf_op jit(solution)/shard_map/ppermute | solution.py:12
  20.8 4.2 %collective-permute-start.3 = (bf16[4,3584]{1,0:T(4,128)(2,1)S(1)}, bf16[4,3584]{1,0:T(4,128)(2,1)S(1)}, u32[]{:S(2)}, u32[]{:S(2)}) collective-permute-start(bf16[4,3584]{1,0:T(4,128)(2,1)S(1)} %collective-permute-done.2), channel_id=1, source_target_pairs={{0,1},{1,2},{2,3},{3,4},{4,5},{5,6},{6,7},{7,0},{8,9},{9,10},{10,1... | collective-permute-start | bytes 86024 | tf_op jit(solution)/shard_map/ppermute | solution.py:12
  25.0 4.2 %collective-permute-start.4 = (bf16[4,3584]{1,0:T(4,128)(2,1)S(1)}, bf16[4,3584]{1,0:T(4,128)(2,1)S(1)}, u32[]{:S(2)}, u32[]{:S(2)}) collective-permute-start(bf16[4,3584]{1,0:T(4,128)(2,1)S(1)} %collective-permute-done.3), channel_id=1, source_target_pairs={{0,1},{1,2},{2,3},{3,4},{4,5},{5,6},{6,7},{7,0},{8,9},{9,10},{10,1... | collective-permute-start | bytes 86024 | tf_op jit(solution)/shard_map/ppermute | solution.py:12
  29.2 4.2 %collective-permute-start.5 = (bf16[4,3584]{1,0:T(4,128)(2,1)S(1)}, bf16[4,3584]{1,0:T(4,128)(2,1)S(1)}, u32[]{:S(2)}, u32[]{:S(2)}) collective-permute-start(bf16[4,3584]{1,0:T(4,128)(2,1)S(1)} %collective-permute-done.4), channel_id=1, source_target_pairs={{0,1},{1,2},{2,3},{3,4},{4,5},{5,6},{6,7},{7,0},{8,9},{9,10},{10,1... | collective-permute-start | bytes 86024 | tf_op jit(solution)/shard_map/ppermute | solution.py:12
  31.0 14.1 %copy-start.1 = (bf16[224,3584]{1,0:T(8,128)(2,1)S(1)}, bf16[224,3584]{1,0:T(8,128)(2,1)}, u32[]{:S(2)}) copy-start(bf16[224,3584]{1,0:T(8,128)(2,1)} %param.8) | copy-start | bytes 4816900
  33.4 4.2 %collective-permute-start.6 = (bf16[4,3584]{1,0:T(4,128)(2,1)S(1)}, bf16[4,3584]{1,0:T(4,128)(2,1)S(1)}, u32[]{:S(2)}, u32[]{:S(2)}) collective-permute-start(bf16[4,3584]{1,0:T(4,128)(2,1)S(1)} %collective-permute-done.5), channel_id=1, source_target_pairs={{0,1},{1,2},{2,3},{3,4},{4,5},{5,6},{6,7},{7,0},{8,9},{9,10},{10,1... | collective-permute-start | bytes 86024 | tf_op jit(solution)/shard_map/ppermute | solution.py:12
  45.1 1.2 copy-start.6
  45.1 77.6 %copy-start.4 = (f32[3584]{0:T(1024)S(1)}, f32[3584]{0:T(1024)}, u32[]{:S(2)}) copy-start(f32[3584]{0:T(1024)} %param.9) | copy-start | bytes 43012
  123.3 13.6 %copy-start.3 = (f32[4,3584]{1,0:T(4,128)}, f32[4,3584]{1,0:T(4,128)S(1)}, u32[]{:S(2)}) copy-start(f32[4,3584]{1,0:T(4,128)S(1)} %get-tuple-element.11) | copy-start | bytes 172036
Sparse Core Ops, SparseCore 0:
  46.4 55.7 all-reduce.3
